TPU v7x, 256 devices: a whole 4x4x8 slice. The times are simulated.
256 devices in a mesh: ctx: 32 (over y, x, core), seq: 8 (over z).
Axes of the slice: x: 4, y: 4, z: 8, core: 2. Of those that a mesh axis runs over, the one named last changes fastest.
Arguments:
- queries: bfloat16 [32768, 4096], P(('seq', 'ctx')), may hold values from -6 to 6
- key_proj: bfloat16 [32768, 4096], P(('seq', 'ctx')), may hold values from -6 to 6
- value_proj: bfloat16 [32768, 4096], P(('seq', 'ctx')), may hold values from -6 to 6
- decay_rate: float32 [16, 4096], P(None, 'ctx'), may hold values from 3.0517578e-06 to 0.06
- residue: float32 [16, 4096], P(None, 'ctx'), may hold values from -1 to 1
- skip_gain: float32 [4096], P('ctx'), may hold values from -1 to 1
Outputs:
- operator_out: bfloat16 [32768, 4096], P(('seq', 'ctx'))
All inputs are finite; a program needn't handle non-finite values.
Results may differ from a plain program's by a relative error of at most 0.011.
Values may be sent and summed in bfloat16 or wider, within the bound.
No kernel may reach another device: no remote copies, remote signals or barrier semaphores. Data moves between devices by JAX's collectives and lax.ppermute only.
A program may use at most 320 MiB of HBM per device.

v0:
```python
import functools

import jax
import jax.numpy as jnp
from jax import lax
from jax.experimental import pallas as pl
from jax.experimental.pallas import tpu as pltpu
from jax.sharding import PartitionSpec as P

F32, BF16 = jnp.float32, jnp.bfloat16
LANES = 128
SUB = 8
CHUNK = 128
SEGS = 8
STEPS = CHUNK // SEGS
MODES = 16
ROWS = CHUNK + 4 * MODES


def one_minus_exp(x):
    series = jnp.ones_like(x)
    for order in range(9, 1, -1):
        series = 1.0 - x * (1.0 / order) * series
    return jnp.where(x < 0.5, x * series, 1.0 - jnp.exp(-x))


def pack_kernel(k_ref, v_ref, rate_ref, resid_ref, gain_ref, out_ref, par, taps):
    @pl.when(pl.program_id(0) == 0)
    def _():
        rate = rate_ref[...]
        weight = resid_ref[...] * jnp.sqrt(one_minus_exp(2.0 * rate))
        power = jnp.exp(-rate)
        high = rate.astype(BF16)
        term = weight
        for lag in range(STEPS):
            tap = jnp.sum(term, axis=0, keepdims=True)
            taps[lag : lag + 1, :] = tap + gain_ref[...] if lag == 0 else tap
            term = term * power
        par[0:16, :] = high
        par[16:32, :] = (rate - high.astype(F32)).astype(BF16)
        par[32:48, :] = weight.astype(BF16)
        par[48:64, :] = taps[...].astype(BF16)

    for g in range(out_ref.shape[0]):
        cols = slice(g * LANES, (g + 1) * LANES)
        out_ref[g, 0:CHUNK, :] = (k_ref[:, cols].astype(F32) * v_ref[:, cols].astype(F32)).astype(BF16)
        out_ref[g, CHUNK:ROWS, :] = par[...]


def states_kernel(in_ref, rate_ref, before_ref, end_ref, sig, ends):
    step = pl.program_id(0)
    nchunks = before_ref.shape[0]
    for i in range(SUB):
        sig[i * CHUNK : (i + 1) * CHUNK, :] = in_ref[i].astype(F32)
    power = jnp.exp(-rate_ref[...])
    powers = [jnp.broadcast_to(power[m : m + 1, :], (SUB, LANES)) for m in range(MODES)]

    def token(t, states):
        x = sig[pl.ds(t, SUB, stride=CHUNK), :]
        return tuple(powers[m] * states[m] + x for m in range(MODES))

    zero = jnp.zeros((SUB, LANES), F32)
    states = lax.fori_loop(0, CHUNK, token, (zero,) * MODES, unroll=8)
    for m in range(MODES):
        ends[pl.ds(pl.multiple_of(m * nchunks + step * SUB, SUB), SUB), :] = states[m]

    @pl.when(step == pl.num_programs(0) - 1)
    def _():
        decay = jnp.exp(-float(CHUNK) * rate_ref[...])
        state = jnp.zeros((MODES, LANES), F32)
        for d in range(nchunks):
            before_ref[d] = state
            state = decay * state + ends[pl.ds(d, MODES, stride=nchunks), :]
        end_ref[...] = state


def inner_kernel(send_ref, par_ref, after_ref, y_ref, seg_ref, sig, ends):
    def group(g, carry):
        sig[...] = send_ref[g].astype(F32)
        rate = par_ref[g, 0:16, :].astype(F32) + par_ref[g, 16:32, :].astype(F32)
        weight = par_ref[g, 32:48, :].astype(F32)
        taps = par_ref[g, 48:64, :].astype(F32)
        power = jnp.exp(-rate)
        xs = [sig[pl.ds(t, SEGS, stride=STEPS), :] for t in range(STEPS)]
        tap = [jnp.broadcast_to(taps[j : j + 1, :], (SEGS, LANES)) for j in range(STEPS)]
        for t in range(STEPS):
            acc = tap[0] * xs[t]
            for j in range(1, t + 1):
                acc = acc + tap[j] * xs[t - j]
            y_ref[g, t] = acc
        for m in range(MODES):
            a = jnp.broadcast_to(power[m : m + 1, :], (SEGS, LANES))
            state = xs[0]
            for t in range(1, STEPS):
                state = a * state + xs[t]
            ends[m * SEGS : (m + 1) * SEGS, :] = state
        decay = jnp.exp(-float(STEPS) * rate)
        lift = weight * power
        state = jnp.zeros((MODES, LANES), F32)
        for i in range(SEGS):
            seg_ref[g, i] = lift * state
            state = decay * state + ends[pl.ds(i, MODES, stride=SEGS), :]
        return carry

    lax.fori_loop(0, send_ref.shape[0], group, 0)


def link_kernel(place_ref, before_ref, blocks_ref, rate_ref, out_ref):
    nchunks = before_ref.shape[0]
    place = place_ref[0]
    span = jnp.exp(-float(CHUNK * nchunks) * rate_ref[...])
    start = jnp.zeros((MODES, LANES), F32)
    for z in range(blocks_ref.shape[0]):
        start = jnp.where(z < place, span * start + blocks_ref[z], start)
    decay = jnp.exp(-float(CHUNK) * rate_ref[...])
    for d in range(nchunks):
        out_ref[d] = (before_ref[d] + start).astype(BF16)
        start = decay * start


def final_kernel(start_ref, par_ref, y_ref, seg_ref, q_ref, out_ref, segs, pre):
    for g in range(y_ref.shape[0]):
        rate = par_ref[g, 0:16, :].astype(F32) + par_ref[g, 16:32, :].astype(F32)
        weight = par_ref[g, 32:48, :].astype(F32)
        power = jnp.exp(-rate)
        decay = jnp.exp(-float(STEPS) * rate)
        lifted = weight * power * start_ref[g].astype(F32)
        for i in range(SEGS):
            segs[pl.ds(i, MODES, stride=SEGS), :] = seg_ref[g, i] + lifted
            lifted = lifted * decay
        terms = [segs[m * SEGS : (m + 1) * SEGS, :] for m in range(MODES)]
        powers = [jnp.broadcast_to(power[m : m + 1, :], (SEGS, LANES)) for m in range(MODES)]
        for t in range(STEPS):
            layer = list(terms)
            while len(layer) > 1:
                layer = [layer[i] + layer[i + 1] for i in range(0, len(layer), 2)]
            pre[pl.ds(t, SEGS, stride=STEPS), :] = y_ref[g, t] + layer[0]
            if t < STEPS - 1:
                terms = [terms[m] * powers[m] for m in range(MODES)]
        cols = slice(g * LANES, (g + 1) * LANES)
        gate = pre[...].astype(BF16).astype(F32)
        out_ref[:, cols] = (q_ref[:, cols].astype(F32) * gate).astype(BF16)


def cost(flops, nbytes):
    return pl.CostEstimate(flops=flops, bytes_accessed=nbytes, transcendentals=0)


def local(queries, key_proj, value_proj, decay_rate, residue, skip_gain, *, interpret=False):
    tokens, channels = queries.shape
    groups = channels // LANES
    per = 8
    grid = groups // per
    full = pl.BlockSpec((MODES, LANES), lambda i: (0, 0))
    wide = pl.BlockSpec((CHUNK, per * LANES), lambda i: (0, i))
    state4 = jax.ShapeDtypeStruct((groups, MODES, LANES), F32)

    send = pl.pallas_call(
        pack_kernel,
        grid=(grid,),
        in_specs=[wide, wide, full, full, pl.BlockSpec((1, LANES), lambda i: (0, 0))],
        out_specs=pl.BlockSpec((per, ROWS, LANES), lambda i: (i, 0, 0)),
        out_shape=jax.ShapeDtypeStruct((groups, ROWS, LANES), BF16),
        scratch_shapes=[pltpu.VMEM((4 * MODES, LANES), BF16), pltpu.VMEM((STEPS, LANES), F32)],
        cost_estimate=cost(1_000_000, 4_000_000),
        interpret=interpret,
        name="pack",
    )(key_proj, value_proj, decay_rate, residue, skip_gain[None, :])

    got = lax.all_to_all(send, "ctx", split_axis=0, concat_axis=0, tiled=True)

    before, end_state = pl.pallas_call(
        states_kernel,
        grid=(groups // SUB,),
        in_specs=[pl.BlockSpec((SUB, CHUNK, LANES), lambda i: (i, 0, 0)), full],
        out_specs=[pl.BlockSpec((groups, MODES, LANES), lambda i: (0, 0, 0)), full],
        out_shape=[state4, jax.ShapeDtypeStruct((MODES, LANES), F32)],
        scratch_shapes=[
            pltpu.VMEM((SUB * CHUNK, LANES), F32),
            pltpu.VMEM((MODES * groups, LANES), F32),
        ],
        cost_estimate=cost(20_000_000, 1_300_000),
        interpret=interpret,
        name="states",
    )(got, decay_rate)

    nseq = lax.axis_size("seq")
    blocks = lax.all_to_all(
        jnp.broadcast_to(end_state[None], (nseq, MODES, LANES)),
        "seq", split_axis=0, concat_axis=0, tiled=True,
    )

    par_spec = pl.BlockSpec((per, 4 * MODES, LANES), lambda i: (i, 2, 0))
    quad = pl.BlockSpec((per, STEPS, SEGS, LANES), lambda i: (i, 0, 0, 0))
    segq = pl.BlockSpec((per, SEGS, MODES, LANES), lambda i: (i, 0, 0, 0))
    inner, seg_states = pl.pallas_call(
        inner_kernel,
        grid=(grid,),
        in_specs=[pl.BlockSpec((per, CHUNK, LANES), lambda i: (i, 0, 0)), par_spec, full],
        out_specs=[quad, segq],
        out_shape=[
            jax.ShapeDtypeStruct((groups, STEPS, SEGS, LANES), F32),
            jax.ShapeDtypeStruct((groups, SEGS, MODES, LANES), F32),
        ],
        scratch_shapes=[pltpu.VMEM((CHUNK, LANES), F32), pltpu.VMEM((MODES * SEGS, LANES), F32)],
        cost_estimate=cost(2_000_000_000, 6_000_000),
        interpret=interpret,
        name="inner",
    )(send, got, end_state)

    place = lax.axis_index("seq").astype(jnp.int32)[None]
    starts = pl.pallas_call(
        link_kernel,
        in_specs=[
            pl.BlockSpec(memory_space=pltpu.SMEM),
            pl.BlockSpec((groups, MODES, LANES), lambda: (0, 0, 0)),
            pl.BlockSpec((nseq, MODES, LANES), lambda: (0, 0, 0)),
            pl.BlockSpec((MODES, LANES), lambda: (0, 0)),
        ],
        out_specs=pl.BlockSpec((groups, MODES, LANES), lambda: (0, 0, 0)),
        out_shape=jax.ShapeDtypeStruct((groups, MODES, LANES), BF16),
        cost_estimate=cost(300_000, 500_000),
        interpret=interpret,
        name="link",
    )(place, before, blocks, decay_rate)

    mine = lax.all_to_all(starts, "ctx", split_axis=0, concat_axis=0, tiled=True)

    return pl.pallas_call(
        final_kernel,
        grid=(grid,),
        in_specs=[
            pl.BlockSpec((per, MODES, LANES), lambda i: (i, 0, 0)), par_spec, quad, segq, wide,
        ],
        out_specs=wide,
        out_shape=jax.ShapeDtypeStruct((tokens, channels), BF16),
        scratch_shapes=[pltpu.VMEM((MODES * SEGS, LANES), F32), pltpu.VMEM((CHUNK, LANES), F32)],
        cost_estimate=cost(20_000_000, 7_000_000),
        interpret=interpret,
        name="final",
    )(mine, got, inner, seg_states, queries)


def solution(mesh):
    rows = P(("seq", "ctx"), None)
    return jax.shard_map(
        local,
        mesh=mesh,
        in_specs=(rows, rows, rows, P(None, "ctx"), P(None, "ctx"), P("ctx")),
        out_specs=rows,
        check_vma=False,
    )
```

profile of v0, /device:TPU:1, one launch (start us, length us, event | category | flops | bytes accessed | tf_op | source)
XLA Modules:
  0.0 79.5 jit_solution(8978218685168578956)
XLA Ops:
  0.0 3.8 %pack.1.send_ref = bf16[32,192,128]{2,1,0:T(8,128)(2,1)} custom-call(bf16[128,4096]{1,0:T(8,128)(2,1)} %k_ref.1, bf16[128,4096]{1,0:T(8,128)(2,1)} %v_ref.1, f32[16,128]{1,0:T(8,128)} %rate_ref.5, f32[16,128]{1,0:T(8,128)} %resid_ref.1, f32[1,128]{1,0:T(1,128)} %bitcast.2), custom_call_target="tpu_custom_call" | custom-call | flops 1000000 | bytes 4000000 | tf_op jit(solution)/shard_map/pack/pallas_call | solution.py:158
  3.8 31.5 %all_to_all.15.in_ref.par_ref = bf16[32,192,128]{2,1,0:T(8,128)(2,1)} all-to-all(bf16[32,192,128]{2,1,0:T(8,128)(2,1)} %pack.1.send_ref), channel_id=1, replica_groups=mesh['ctx'=32,'seq'=8] {'ctx'}, dimensions={0} | all-to-all | bytes 3145728 | tf_op jit(solution)/shard_map/all_to_all | solution.py:170
  35.3 5.3 %states.1 = (f32[32,16,128]{2,1,0:T(8,128)}, f32[16,128]{1,0:T(8,128)}) custom-call(bf16[32,192,128]{2,1,0:T(8,128)(2,1)} %all_to_all.15.in_ref.par_ref, f32[16,128]{1,0:T(8,128)} %rate_ref.5), custom_call_target="tpu_custom_call" | custom-call | flops 20000000 | bytes 1300000 | tf_op jit(solution)/shard_map/states/pallas_call | solution.py:172
  40.6 1.3 %broadcast_in_dim.14 = f32[8,16,128]{2,1,0:T(8,128)} broadcast(f32[16,128]{1,0:T(8,128)} %get-tuple-element.10.after_ref), dimensions={1,2} | broadcast | bytes 73728 | tf_op jit(solution)/shard_map/broadcast_in_dim | solution.py:189
  41.9 8.2 %all-to-all-start.1 = ((f32[8,16,128]{2,1,0:T(8,128)}), f32[8,16,128]{2,1,0:T(8,128)S(1)}, u32[]{:S(2)}, u32[]{:S(2)}) async-start(f32[8,16,128]{2,1,0:T(8,128)} %broadcast_in_dim.14), calls=%async_computation.1 | async-start | bytes 131072 | tf_op jit(solution)/shard_map/all_to_all | solution.py:188
  50.1 7.2 %all-to-all-done.1.blocks_ref = f32[8,16,128]{2,1,0:T(8,128)S(1)} async-done(((f32[8,16,128]{2,1,0:T(8,128)}), f32[8,16,128]{2,1,0:T(8,128)S(1)}, u32[]{:S(2)}, u32[]{:S(2)}) %all-to-all-start.1) | async-done | bytes 65568 | tf_op jit(solution)/shard_map/all_to_all | solution.py:188
  57.4 0.0 copy-start.1
  57.4 0.6 copy-done.1
  58.0 1.7 %link.1 = bf16[32,16,128]{2,1,0:T(8,128)(2,1)} custom-call(s32[1]{0:T(128)} %bitcast.place_ref, f32[32,16,128]{2,1,0:T(8,128)} %get-tuple-element.9.before_ref, f32[8,16,128]{2,1,0:T(8,128)} %copy-done.1, f32[16,128]{1,0:T(8,128)} %rate_ref.5), custom_call_target="tpu_custom_call" | custom-call | flops 300000 | bytes 500000 | tf_op jit(solution)/shard_map/link/pallas_call | solution.py:212
  59.7 5.4 %all-to-all-start.2 = ((bf16[32,16,128]{2,1,0:T(8,128)(2,1)}), bf16[32,16,128]{2,1,0:T(8,128)(2,1)S(1)}, u32[]{:S(2)}, u32[]{:S(2)}) async-start(bf16[32,16,128]{2,1,0:T(8,128)(2,1)} %link.1), calls=%async_computation.2 | async-start | bytes 262144 | tf_op jit(solution)/shard_map/all_to_all | solution.py:227
  65.1 7.0 %inner.1 = (f32[32,16,8,128]{3,2,1,0:T(8,128)}, f32[32,8,16,128]{3,2,1,0:T(8,128)}) custom-call(bf16[32,192,128]{2,1,0:T(8,128)(2,1)} %pack.1.send_ref, bf16[32,192,128]{2,1,0:T(8,128)(2,1)} %all_to_all.15.in_ref.par_ref, f32[16,128]{1,0:T(8,128)} %get-tuple-element.10.after_ref), custom_call_target="tpu_custom_call" | custom-call | flops 2000000000 | bytes 6000000 | tf_op jit(solution)/shard_map/inner/pallas_call | solution.py:196
  72.1 0.7 all-to-all-done.2.start_ref
  72.8 0.0 copy-start
  72.8 0.7 copy-done
  73.5 6.1 %final.1 = bf16[128,4096]{1,0:T(8,128)(2,1)} custom-call(bf16[32,16,128]{2,1,0:T(8,128)(2,1)} %copy-done, bf16[32,192,128]{2,1,0:T(8,128)(2,1)} %all_to_all.15.in_ref.par_ref, f32[32,16,8,128]{3,2,1,0:T(8,128)} %get-tuple-element.11.y_ref, f32[32,8,16,128]{3,2,1,0:T(8,128)} %get-tuple-element.12.seg_ref, bf16[128,4096]{1,0:T(8,128)(2,1)} %q_ref.1), custom_call_target="tpu_custom_call" | custom-call | flops 20000000 | bytes 7000000 | tf_op jit(solution)/shard_map/final/pallas_call | solution.py:229
Async XLA Ops:
  41.9 15.4 %all-to-all-start.1 = ((f32[8,16,128]{2,1,0:T(8,128)}), f32[8,16,128]{2,1,0:T(8,128)S(1)}, u32[]{:S(2)}, u32[]{:S(2)}) async-start(f32[8,16,128]{2,1,0:T(8,128)} %broadcast_in_dim.14), calls=%async_computation.1 | async-start | bytes 131072 | tf_op jit(solution)/shard_map/all_to_all | solution.py:188
  57.4 0.6 copy-start.1
  59.7 13.1 %all-to-all-start.2 = ((bf16[32,16,128]{2,1,0:T(8,128)(2,1)}), bf16[32,16,128]{2,1,0:T(8,128)(2,1)S(1)}, u32[]{:S(2)}, u32[]{:S(2)}) async-start(bf16[32,16,128]{2,1,0:T(8,128)(2,1)} %link.1), calls=%async_computation.2 | async-start | bytes 262144 | tf_op jit(solution)/shard_map/all_to_all | solution.py:227
  72.8 0.7 copy-start
where the time goes:
time: 80.2 us; the launch traced here: 79.5 us
  blocking collectives  31.5 us (39%)
  Pallas kernels  24 us (30%)
  starting transfers between devices  13.6 us (17%)
  waiting for transfers between devices  7.93 us (10%)
  local copies, waits for them, and re-layouts  2.59 us (3%)
    all_to_all x1, blocking collectives, local(): got = lax.all_to_all(send, 'ctx', split_axis=0, concat_axis=0, tiled=True)  31.5 us
    all_to_all x1, starting transfers between devices, local(): lax.all_to_all(jnp.broadcast_to(end_state[None], (nseq, MODES, LANES)), '...  8.19 us
    all_to_all x1, waiting for transfers between devices, local(): lax.all_to_all(jnp.broadcast_to(end_state[None], (nseq, MODES, LANES)), '...  7.24 us
    pallas_call x1, Pallas kernels, local(): pl.pallas_call(inner_kernel, grid=(grid,), in_specs=[pl.BlockSpec((per, C...  7.04 us
    pallas_call x1, Pallas kernels, local(): pl.pallas_call(final_kernel, grid=(grid,), in_specs=[pl.BlockSpec((per, M...  6.08 us
    all_to_all x1, starting transfers between devices, local(): lax.all_to_all(starts, 'ctx', split_axis=0, concat_axis=0, tiled=True)  5.37 us
    pallas_call x1, Pallas kernels, local(): pl.pallas_call(states_kernel, grid=(groups // SUB,), in_specs=[pl.BlockSp...  5.33 us
    pallas_call x1, Pallas kernels, local(): pl.pallas_call(pack_kernel, grid=(grid,), in_specs=[wide, wide, full, ful...  3.81 us
  transfers between devices with their start and end apart: 2, of which 2 were waited for; matrix products, arithmetic and copies ran while one was open for 0% of the time, Pallas kernels for 9%

commit v1 on v0

--- a/solution.py
+++ b/solution.py
@@ -14,7 +14,7 @@
 SEGS = 8
 STEPS = CHUNK // SEGS
 MODES = 16
-ROWS = CHUNK + 4 * MODES
+TABLE = 3 * MODES + STEPS
 
 
 def one_minus_exp(x):
@@ -24,27 +24,24 @@
     return jnp.where(x < 0.5, x * series, 1.0 - jnp.exp(-x))
 
 
-def pack_kernel(k_ref, v_ref, rate_ref, resid_ref, gain_ref, out_ref, par, taps):
+def pack_kernel(k_ref, v_ref, rate_ref, resid_ref, gain_ref, out_ref, table_ref):
     @pl.when(pl.program_id(0) == 0)
     def _():
         rate = rate_ref[...]
         weight = resid_ref[...] * jnp.sqrt(one_minus_exp(2.0 * rate))
         power = jnp.exp(-rate)
-        high = rate.astype(BF16)
+        table_ref[0:16, :] = power
+        table_ref[16:32, :] = weight * power
+        table_ref[32:48, :] = jnp.exp(-float(STEPS) * rate)
         term = weight
         for lag in range(STEPS):
             tap = jnp.sum(term, axis=0, keepdims=True)
-            taps[lag : lag + 1, :] = tap + gain_ref[...] if lag == 0 else tap
+            table_ref[48 + lag : 49 + lag, :] = tap + gain_ref[...] if lag == 0 else tap
             term = term * power
-        par[0:16, :] = high
-        par[16:32, :] = (rate - high.astype(F32)).astype(BF16)
-        par[32:48, :] = weight.astype(BF16)
-        par[48:64, :] = taps[...].astype(BF16)
 
     for g in range(out_ref.shape[0]):
         cols = slice(g * LANES, (g + 1) * LANES)
-        out_ref[g, 0:CHUNK, :] = (k_ref[:, cols].astype(F32) * v_ref[:, cols].astype(F32)).astype(BF16)
-        out_ref[g, CHUNK:ROWS, :] = par[...]
+        out_ref[g] = (k_ref[:, cols].astype(F32) * v_ref[:, cols].astype(F32)).astype(BF16)
 
 
 def states_kernel(in_ref, rate_ref, before_ref, end_ref, sig, ends):
@@ -71,16 +68,15 @@
         for d in range(nchunks):
             before_ref[d] = state
             state = decay * state + ends[pl.ds(d, MODES, stride=nchunks), :]
-        end_ref[...] = state
-
-
-def inner_kernel(send_ref, par_ref, after_ref, y_ref, seg_ref, sig, ends):
+        for z in range(end_ref.shape[0]):
+            end_ref[z] = state
+
+
+def inner_kernel(send_ref, par_ref, y_ref, seg_ref, sig, ends):
     def group(g, carry):
         sig[...] = send_ref[g].astype(F32)
-        rate = par_ref[g, 0:16, :].astype(F32) + par_ref[g, 16:32, :].astype(F32)
-        weight = par_ref[g, 32:48, :].astype(F32)
-        taps = par_ref[g, 48:64, :].astype(F32)
-        power = jnp.exp(-rate)
+        power = par_ref[g, 0:16, :]
+        taps = par_ref[g, 48:64, :]
         xs = [sig[pl.ds(t, SEGS, stride=STEPS), :] for t in range(STEPS)]
         tap = [jnp.broadcast_to(taps[j : j + 1, :], (SEGS, LANES)) for j in range(STEPS)]
         for t in range(STEPS):
@@ -94,8 +90,8 @@
             for t in range(1, STEPS):
                 state = a * state + xs[t]
             ends[m * SEGS : (m + 1) * SEGS, :] = state
-        decay = jnp.exp(-float(STEPS) * rate)
-        lift = weight * power
+        lift = par_ref[g, 16:32, :]
+        decay = par_ref[g, 32:48, :]
         state = jnp.zeros((MODES, LANES), F32)
         for i in range(SEGS):
             seg_ref[g, i] = lift * state
@@ -120,11 +116,9 @@
 
 def final_kernel(start_ref, par_ref, y_ref, seg_ref, q_ref, out_ref, segs, pre):
     for g in range(y_ref.shape[0]):
-        rate = par_ref[g, 0:16, :].astype(F32) + par_ref[g, 16:32, :].astype(F32)
-        weight = par_ref[g, 32:48, :].astype(F32)
-        power = jnp.exp(-rate)
-        decay = jnp.exp(-float(STEPS) * rate)
-        lifted = weight * power * start_ref[g].astype(F32)
+        power = par_ref[g, 0:16, :]
+        decay = par_ref[g, 32:48, :]
+        lifted = par_ref[g, 16:32, :] * start_ref[g].astype(F32)
         for i in range(SEGS):
             segs[pl.ds(i, MODES, stride=SEGS), :] = seg_ref[g, i] + lifted
             lifted = lifted * decay
@@ -150,53 +144,60 @@
     tokens, channels = queries.shape
     groups = channels // LANES
     per = 8
+    params = pltpu.CompilerParams(vmem_limit_bytes=16 * 1024 * 1024)
     grid = groups // per
     full = pl.BlockSpec((MODES, LANES), lambda i: (0, 0))
     wide = pl.BlockSpec((CHUNK, per * LANES), lambda i: (0, i))
     state4 = jax.ShapeDtypeStruct((groups, MODES, LANES), F32)
 
-    send = pl.pallas_call(
+    nseq = lax.axis_size("seq")
+    tile = pl.BlockSpec((per, CHUNK, LANES), lambda i: (i, 0, 0))
+
+    send, table = pl.pallas_call(
         pack_kernel,
         grid=(grid,),
         in_specs=[wide, wide, full, full, pl.BlockSpec((1, LANES), lambda i: (0, 0))],
-        out_specs=pl.BlockSpec((per, ROWS, LANES), lambda i: (i, 0, 0)),
-        out_shape=jax.ShapeDtypeStruct((groups, ROWS, LANES), BF16),
-        scratch_shapes=[pltpu.VMEM((4 * MODES, LANES), BF16), pltpu.VMEM((STEPS, LANES), F32)],
+        out_specs=[tile, pl.BlockSpec((TABLE, LANES), lambda i: (0, 0))],
+        out_shape=[
+            jax.ShapeDtypeStruct((groups, CHUNK, LANES), BF16),
+            jax.ShapeDtypeStruct((TABLE, LANES), F32),
+        ],
         cost_estimate=cost(1_000_000, 4_000_000),
         interpret=interpret,
         name="pack",
     )(key_proj, value_proj, decay_rate, residue, skip_gain[None, :])
 
+    tables = lax.all_gather(table, "ctx", axis=0)
     got = lax.all_to_all(send, "ctx", split_axis=0, concat_axis=0, tiled=True)
 
     before, end_state = pl.pallas_call(
         states_kernel,
         grid=(groups // SUB,),
         in_specs=[pl.BlockSpec((SUB, CHUNK, LANES), lambda i: (i, 0, 0)), full],
-        out_specs=[pl.BlockSpec((groups, MODES, LANES), lambda i: (0, 0, 0)), full],
-        out_shape=[state4, jax.ShapeDtypeStruct((MODES, LANES), F32)],
+        out_specs=[
+            pl.BlockSpec((groups, MODES, LANES), lambda i: (0, 0, 0)),
+            pl.BlockSpec((nseq, MODES, LANES), lambda i: (0, 0, 0)),
+        ],
+        out_shape=[state4, jax.ShapeDtypeStruct((nseq, MODES, LANES), F32)],
         scratch_shapes=[
             pltpu.VMEM((SUB * CHUNK, LANES), F32),
             pltpu.VMEM((MODES * groups, LANES), F32),
         ],
         cost_estimate=cost(20_000_000, 1_300_000),
+        compiler_params=params,
         interpret=interpret,
         name="states",
     )(got, decay_rate)
 
-    nseq = lax.axis_size("seq")
-    blocks = lax.all_to_all(
-        jnp.broadcast_to(end_state[None], (nseq, MODES, LANES)),
-        "seq", split_axis=0, concat_axis=0, tiled=True,
-    )
-
-    par_spec = pl.BlockSpec((per, 4 * MODES, LANES), lambda i: (i, 2, 0))
+    blocks = lax.all_to_all(end_state, "seq", split_axis=0, concat_axis=0, tiled=True)
+
+    par_spec = pl.BlockSpec((per, TABLE, LANES), lambda i: (i, 0, 0))
     quad = pl.BlockSpec((per, STEPS, SEGS, LANES), lambda i: (i, 0, 0, 0))
     segq = pl.BlockSpec((per, SEGS, MODES, LANES), lambda i: (i, 0, 0, 0))
     inner, seg_states = pl.pallas_call(
         inner_kernel,
         grid=(grid,),
-        in_specs=[pl.BlockSpec((per, CHUNK, LANES), lambda i: (i, 0, 0)), par_spec, full],
+        in_specs=[tile, par_spec],
         out_specs=[quad, segq],
         out_shape=[
             jax.ShapeDtypeStruct((groups, STEPS, SEGS, LANES), F32),
@@ -206,7 +207,7 @@
         cost_estimate=cost(2_000_000_000, 6_000_000),
         interpret=interpret,
         name="inner",
-    )(send, got, end_state)
+    )(send, tables)
 
     place = lax.axis_index("seq").astype(jnp.int32)[None]
     starts = pl.pallas_call(
@@ -220,6 +221,7 @@
         out_specs=pl.BlockSpec((groups, MODES, LANES), lambda: (0, 0, 0)),
         out_shape=jax.ShapeDtypeStruct((groups, MODES, LANES), BF16),
         cost_estimate=cost(300_000, 500_000),
+        compiler_params=params,
         interpret=interpret,
         name="link",
     )(place, before, blocks, decay_rate)
@@ -238,7 +240,7 @@
         cost_estimate=cost(20_000_000, 7_000_000),
         interpret=interpret,
         name="final",
-    )(mine, got, inner, seg_states, queries)
+    )(mine, tables, inner, seg_states, queries)
 
 
 def solution(mesh):

time: 80.2 us -> 86 us (1.072)
  between operations: 0.02 us -> 13.4 us
  blocking collectives: 31.5 us -> 26 us
  Pallas kernels: 24 us -> 21.6 us
  waiting for transfers between devices: 7.93 us -> 10.1 us
  local copies, waits for them, and re-layouts: 2.59 us -> 0.65 us
    all_to_all x1, blocking collectives: 31.5 us -> 26 us  [local(): got = lax.all_to_all(send, 'ctx', split_axis=0, concat_axis=0, tiled=True)]
    all_gather x0 -> x1, waiting for transfers between devices: none -> 2.89 us  [local(): tables = lax.all_gather(table, 'ctx', axis=0)]
    broadcast_in_dim x1 -> x0, local copies, waits for them, and re-layouts: 1.32 us -> none  [local(): jnp.broadcast_to(end_state[None], (nseq, MODES, LANES))]
    pallas_call x1, Pallas kernels: 5.33 us -> 4.12 us  [local(): pl.pallas_call(states_kernel, grid=(groups // SUB,), in_specs=[pl.BlockSp...]
    pallas_call x1, Pallas kernels: 1.7 us -> 0.71 us  [local(): pl.pallas_call(link_kernel, in_specs=[pl.BlockSpec(memory_space=pltpu.SME...]
  transfers between devices with their start and end apart: 2 -> 3, of which waited for: 2 -> 2; matrix products, arithmetic and copies ran while one was open for 0% -> 0% of each run, Pallas kernels for 9% -> 14%
where the time goes in v1:
time: 86 us; the launch traced here: 85.5 us
  blocking collectives  26 us (30%)
  Pallas kernels  21.6 us (25%)
  starting transfers between devices  13.6 us (16%)
  between operations  13.4 us (16%)
  waiting for transfers between devices  10.1 us (12%)
    all_to_all x1, blocking collectives, local(): got = lax.all_to_all(send, 'ctx', split_axis=0, concat_axis=0, tiled=True)  26 us
    all_to_all x1, starting transfers between devices, local(): lax.all_to_all(end_state, 'seq', split_axis=0, concat_axis=0, tiled=True)  7.69 us
    all_to_all x1, waiting for transfers between devices, local(): lax.all_to_all(end_state, 'seq', split_axis=0, concat_axis=0, tiled=True)  7.23 us
    pallas_call x1, Pallas kernels, local(): pl.pallas_call(inner_kernel, grid=(grid,), in_specs=[tile, par_spec], out...  7 us
    pallas_call x1, Pallas kernels, local(): pl.pallas_call(final_kernel, grid=(grid,), in_specs=[pl.BlockSpec((per, M...  5.99 us
    all_to_all x1, starting transfers between devices, local(): lax.all_to_all(starts, 'ctx', split_axis=0, concat_axis=0, tiled=True)  5.96 us
    pallas_call x1, Pallas kernels, local(): pl.pallas_call(states_kernel, grid=(groups // SUB,), in_specs=[pl.BlockSp...  4.12 us
    pallas_call x1, Pallas kernels, local(): pl.pallas_call(pack_kernel, grid=(grid,), in_specs=[wide, wide, full, ful...  3.78 us
  transfers between devices with their start and end apart: 3, of which 2 were waited for; matrix products, arithmetic and copies ran while one was open for 0% of the time, Pallas kernels for 14%

profile of v1, /device:TPU:1, one launch (start us, length us, event | category | flops | bytes accessed | tf_op | source)
XLA Modules:
  0.0 85.5 jit_solution(14573335692446928952)
XLA Ops:
  6.5 0.0 all-gather.3.cloned.1.call-start
  6.5 0.0 copy-start
  6.5 3.8 %pack.1 = (bf16[32,128,128]{2,1,0:T(8,128)(2,1)}, f32[64,128]{1,0:T(8,128)}) custom-call(bf16[128,4096]{1,0:T(8,128)(2,1)} %k_ref.1, bf16[128,4096]{1,0:T(8,128)(2,1)} %v_ref.1, f32[16,128]{1,0:T(8,128)} %rate_ref.5, f32[16,128]{1,0:T(8,128)} %resid_ref.1, f32[1,128]{1,0:T(1,128)} %bitcast.5), custom_call_target="tpu_custom_call" | custom-call | flops 1000000 | bytes 4000000 | tf_op jit(solution)/shard_map/pack/pallas_call | solution.py:156
  10.3 0.0 all-gather.3.cloned.1.call-update
  10.3 26.0 %all_to_all.15.in_ref = bf16[32,128,128]{2,1,0:T(8,128)(2,1)S(1)} all-to-all(bf16[32,128,128]{2,1,0:T(8,128)(2,1)} %get-tuple-element.11.send_ref), channel_id=1, replica_groups=mesh['ctx'=32,'seq'=8] {'ctx'}, dimensions={0} | all-to-all | bytes 2097152 | tf_op jit(solution)/shard_map/all_to_all | solution.py:171
  36.4 0.0 copy-done
  36.4 4.1 %states.1 = (f32[32,16,128]{2,1,0:T(8,128)S(1)}, f32[8,16,128]{2,1,0:T(8,128)}) custom-call(bf16[32,128,128]{2,1,0:T(8,128)(2,1)S(1)} %all_to_all.15.in_ref, f32[16,128]{1,0:T(8,128)S(1)} %copy-done), custom_call_target="tpu_custom_call" | custom-call | flops 20000000 | bytes 1300000 | tf_op jit(solution)/shard_map/states/pallas_call | solution.py:173
  40.5 7.7 %all-to-all-start.1 = ((f32[8,16,128]{2,1,0:T(8,128)}), f32[8,16,128]{2,1,0:T(8,128)S(1)}, u32[]{:S(2)}, u32[]{:S(2)}) async-start(f32[8,16,128]{2,1,0:T(8,128)} %get-tuple-element.13), calls=%async_computation.1 | async-start | bytes 131072 | tf_op jit(solution)/shard_map/all_to_all | solution.py:192
  48.2 7.2 %all-to-all-done.1.blocks_ref = f32[8,16,128]{2,1,0:T(8,128)S(1)} async-done(((f32[8,16,128]{2,1,0:T(8,128)}), f32[8,16,128]{2,1,0:T(8,128)S(1)}, u32[]{:S(2)}, u32[]{:S(2)}) %all-to-all-start.1) | async-done | bytes 65568 | tf_op jit(solution)/shard_map/all_to_all | solution.py:192
  55.4 0.7 link.1
  56.1 6.0 %all-to-all-start.2 = ((bf16[32,16,128]{2,1,0:T(8,128)(2,1)}), bf16[32,16,128]{2,1,0:T(8,128)(2,1)S(1)}, u32[]{:S(2)}, u32[]{:S(2)}) async-start(bf16[32,16,128]{2,1,0:T(8,128)(2,1)} %link.1), calls=%async_computation.2 | async-start | bytes 262144 | tf_op jit(solution)/shard_map/all_to_all | solution.py:229
  62.1 2.9 %all-gather.3.cloned.1.call-done = f32[2048,128]{1,0:T(8,128)} async-done(((f32[64,128]{1,0:T(8,128)}), f32[2048,128]{1,0:T(8,128)}) %all-gather.3.cloned.1.call-update) | async-done | bytes 1048592 | tf_op jit(solution)/shard_map/all_gather | solution.py:170
  65.0 7.0 %inner.1 = (f32[32,16,8,128]{3,2,1,0:T(8,128)}, f32[32,8,16,128]{3,2,1,0:T(8,128)}) custom-call(bf16[32,128,128]{2,1,0:T(8,128)(2,1)} %get-tuple-element.11.send_ref, f32[32,64,128]{2,1,0:T(8,128)} %bitcast.3), custom_call_target="tpu_custom_call" | custom-call | flops 2000000000 | bytes 6000000 | tf_op jit(solution)/shard_map/inner/pallas_call | solution.py:197
  72.0 0.0 all-to-all-done.2.start_ref
  72.0 0.0 copy-start.1
  72.0 0.6 copy-done.1
  72.6 6.0 %final.1 = bf16[128,4096]{1,0:T(8,128)(2,1)} custom-call(bf16[32,16,128]{2,1,0:T(8,128)(2,1)} %copy-done.1, f32[32,64,128]{2,1,0:T(8,128)} %bitcast.4, f32[32,16,8,128]{3,2,1,0:T(8,128)} %get-tuple-element.15.y_ref, f32[32,8,16,128]{3,2,1,0:T(8,128)} %get-tuple-element.16.seg_ref, bf16[128,4096]{1,0:T(8,128)(2,1)} %q_ref.1), custom_call_target="tpu_custom_call" | custom-call | flops 20000000 | bytes 7000000 | tf_op jit(solution)/shard_map/final/pallas_call | solution.py:231
Async XLA Ops:
  6.5 58.4 %all-gather.3.cloned.1.call-start = ((), (), s32[]{:S(2)}) async-start(), calls=%async_computation.3 | async-start | bytes 1081344 | tf_op jit(solution)/shard_map/all_gather | solution.py:170
  6.5 29.8 %copy-start = (f32[16,128]{1,0:T(8,128)S(1)}, f32[16,128]{1,0:T(8,128)}, u32[]{:S(2)}) copy-start(f32[16,128]{1,0:T(8,128)} %rate_ref.5) | copy-start | bytes 24580
  40.5 14.9 %all-to-all-start.1 = ((f32[8,16,128]{2,1,0:T(8,128)}), f32[8,16,128]{2,1,0:T(8,128)S(1)}, u32[]{:S(2)}, u32[]{:S(2)}) async-start(f32[8,16,128]{2,1,0:T(8,128)} %get-tuple-element.13), calls=%async_computation.1 | async-start | bytes 131072 | tf_op jit(solution)/shard_map/all_to_all | solution.py:192
  56.1 15.9 %all-to-all-start.2 = ((bf16[32,16,128]{2,1,0:T(8,128)(2,1)}), bf16[32,16,128]{2,1,0:T(8,128)(2,1)S(1)}, u32[]{:S(2)}, u32[]{:S(2)}) async-start(bf16[32,16,128]{2,1,0:T(8,128)(2,1)} %link.1), calls=%async_computation.2 | async-start | bytes 262144 | tf_op jit(solution)/shard_map/all_to_all | solution.py:229
  72.0 0.6 copy-start.1
Sparse Core Ops, SparseCore 0:
  10.5 54.4 all-gather.2
